TPU v7x, 32 devices: a whole 2x2x4 slice. The times are simulated.
32 devices in a mesh: expert: 8 (over z, x), fsdp: 4 (over y, core).
Axes of the slice: x: 2, y: 2, z: 4, core: 2. Of those that a mesh axis runs over, the one named last changes fastest.
Arguments:
- tokens: bfloat16 [160, 197, 512], P(('expert', 'fsdp')), may hold values from -6 to 6
- ln1_gain: bfloat16 [512], P('fsdp'), may hold values from 0.5 to 1.5
- ln1_bias: bfloat16 [512], P('fsdp'), may hold values from -1.796875 to 1.796875
- w_qkv: bfloat16 [512, 1536], P('fsdp'), may hold values from -0.25 to 0.25
- q_bias: bfloat16 [512], P('fsdp'), may hold values from -1.796875 to 1.796875
- v_bias: bfloat16 [512], P('fsdp'), may hold values from -1.796875 to 1.796875
- w_out: bfloat16 [512, 512], P('fsdp'), may hold values from -1.5 to 1.5
- out_bias: bfloat16 [512], P('fsdp'), may hold values from -1.796875 to 1.796875
- ln2_gain: bfloat16 [512], P('fsdp'), may hold values from 0.5 to 1.5
- ln2_bias: bfloat16 [512], P('fsdp'), may hold values from -1.796875 to 1.796875
- w_router: bfloat16 [512, 8], P('fsdp'), may hold values from -0.1875 to 0.1875
- expert_w1: bfloat16 [8, 512, 2048], P('expert', 'fsdp'), may hold values from -0.25 to 0.25
- expert_b1: bfloat16 [8, 2048], P('expert', 'fsdp'), may hold values from -1.796875 to 1.796875
- expert_w2: bfloat16 [8, 2048, 512], P('expert', 'fsdp'), may hold values from -0.75 to 0.75
- expert_b2: bfloat16 [8, 512], P('expert', 'fsdp'), may hold values from -6 to 6
- route_ids: int32 [31520, 2], P(('expert', 'fsdp')), may hold values from 0 to 7, all different within a row; in each aligned block of 985 rows (0 to 984, 985 to 1969, ...) at most 432 rows name the same one
- clip_threshold: int32 [8], replicated, may hold values from 2 to 4
- grad_output: bfloat16 [160, 197, 512], P(('expert', 'fsdp')), may hold values from -6 to 6
Outputs:
- output: bfloat16 [160, 197, 512], P(('expert', 'fsdp'))
- input_grad: float32 [160, 197, 512], P(('expert', 'fsdp'))
- grad_ln1_gain: float32 [512], P('fsdp')
- grad_ln1_bias: float32 [512], P('fsdp')
- grad_w_qkv: float32 [512, 1536], P('fsdp')
- grad_q_bias: float32 [512], P('fsdp')
- grad_v_bias: float32 [512], P('fsdp')
- grad_w_out: float32 [512, 512], P('fsdp')
- grad_out_bias: float32 [512], P('fsdp')
- grad_ln2_gain: float32 [512], P('fsdp')
- grad_ln2_bias: float32 [512], P('fsdp')
- grad_w_router: float32 [512, 8], P('fsdp')
- grad_expert_w1: float32 [8, 512, 2048], P('expert', 'fsdp')
- grad_expert_b1: float32 [8, 2048], P('expert', 'fsdp')
- grad_expert_w2: float32 [8, 2048, 512], P('expert', 'fsdp')
- grad_expert_b2: float32 [8, 512], P('expert', 'fsdp')
- clipped_qkv: bfloat16 [512, 1536], P('fsdp')
Inputs may be any that keep to these rules, and one draw needn't show every extreme that they name: `route_ids`: each row names 2 different experts; among the 985 rows of one device no expert is named by more than 432 rows, and in some device's rows one expert is named by exactly 432.
All inputs are finite; a program needn't handle non-finite values.
Results may differ from a plain program's by a relative error of at most 0.024.
Values may be sent and summed in bfloat16 or wider, within the bound.
No kernel may reach another device: no remote copies, remote signals or barrier semaphores. Data moves between devices by JAX's collectives and lax.ppermute only.
A program may use at most 256 MiB of HBM per device.

v0:
```python
import jax
import jax.numpy as jnp
from jax import lax
from jax.sharding import PartitionSpec as P

HEADS = 8
norm_eps = 1e-06
highest = lax.Precision.HIGHEST


def layer_norm(matrix, norm_gain, norm_shift):
    centred = matrix - jnp.mean(matrix, axis=1, keepdims=True)
    inverse = lax.rsqrt(jnp.mean(centred * centred, axis=1, keepdims=True) + norm_eps)
    normed = centred * inverse
    return (normed * norm_gain + norm_shift, normed, inverse)


def norm_backward(upstream, norm_gain, normed, inverse):
    scaled = upstream * norm_gain
    spread = (
        scaled
        - jnp.mean(scaled, axis=1, keepdims=True)
        - normed * jnp.mean(scaled * normed, axis=1, keepdims=True)
    )
    return (spread * inverse, jnp.sum(upstream * normed, axis=0), jnp.sum(upstream, axis=0))


def gelu_exact(values):
    return jax.nn.gelu(values, approximate=False)


def shards(
    tokens,
    ln1_gain,
    ln1_bias,
    w_qkv,
    q_bias,
    v_bias,
    w_out,
    out_bias,
    ln2_gain,
    ln2_bias,
    w_router,
    expert_w1,
    expert_b1,
    expert_w2,
    expert_b2,
    route_ids,
    clip_threshold,
    grad_output,
):
    gathered = (
        lax.all_gather(ln1_gain, "fsdp", axis=0, tiled=True),
        lax.all_gather(ln1_bias, "fsdp", axis=0, tiled=True),
        lax.all_gather(w_qkv, "fsdp", axis=0, tiled=True),
        lax.all_gather(q_bias, "fsdp", axis=0, tiled=True),
        lax.all_gather(v_bias, "fsdp", axis=0, tiled=True),
        lax.all_gather(w_out, "fsdp", axis=0, tiled=True),
        lax.all_gather(out_bias, "fsdp", axis=0, tiled=True),
        lax.all_gather(ln2_gain, "fsdp", axis=0, tiled=True),
        lax.all_gather(ln2_bias, "fsdp", axis=0, tiled=True),
        lax.all_gather(w_router, "fsdp", axis=0, tiled=True),
        lax.all_gather(expert_w1, "fsdp", axis=1, tiled=True),
        lax.all_gather(expert_b1, "fsdp", axis=1, tiled=True),
        lax.all_gather(expert_w2, "fsdp", axis=1, tiled=True),
        lax.all_gather(expert_b2, "fsdp", axis=1, tiled=True),
    )
    gain_one = gathered[0].astype(jnp.float32)
    shift_one = gathered[1].astype(jnp.float32)
    qkv_weight = gathered[2]
    query_bias = gathered[3].astype(jnp.float32)
    value_bias = gathered[4].astype(jnp.float32)
    out_weight = gathered[5]
    out_shift = gathered[6].astype(jnp.float32)
    gain_two = gathered[7].astype(jnp.float32)
    shift_two = gathered[8].astype(jnp.float32)
    router_weight = gathered[9].astype(jnp.float32)
    first_weight = gathered[10][0]
    first_bias = gathered[11][0].astype(jnp.float32)
    second_weight = gathered[12][0]
    second_bias = gathered[13][0].astype(jnp.float32)
    image_count, sequence, feature_width = tokens.shape
    token_count = image_count * sequence
    head_count = HEADS
    head_size = feature_width // head_count
    score_scale = head_size ** (-0.5)
    route_top = route_ids.shape[1]
    expert_total = router_weight.shape[1]
    capacity = (7 * token_count // (2 * expert_total) + 7) // 8 * 8
    head_shape = (image_count, sequence, head_count, head_size)
    residual = tokens.astype(jnp.float32).reshape(token_count, feature_width)
    normed_in, hat_one, inverse_one = layer_norm(residual, gain_one, shift_one)
    normed_low = normed_in.astype(jnp.bfloat16)
    projected = jnp.dot(normed_low, qkv_weight, preferred_element_type=jnp.float32)
    queries = (projected[:, :feature_width] + query_bias).astype(jnp.bfloat16).reshape(head_shape)
    key_rows = (
        projected[:, feature_width : 2 * feature_width].astype(jnp.bfloat16).reshape(head_shape)
    )
    value_rows = (
        (projected[:, 2 * feature_width :] + value_bias).astype(jnp.bfloat16).reshape(head_shape)
    )
    scores = (
        jnp.einsum("bqhd,bkhd->bhqk", queries, key_rows, preferred_element_type=jnp.float32)
        * score_scale
    )
    head_peak = jnp.max(scores, axis=(0, 2, 3))
    row_top = jnp.max(scores, axis=3, keepdims=True)
    log_total = row_top + jnp.log(jnp.sum(jnp.exp(scores - row_top), axis=3, keepdims=True))
    attn_low = jnp.exp(scores - log_total).astype(jnp.bfloat16)
    mixed_rows = jnp.einsum(
        "bhqk,bkhd->bqhd", attn_low, value_rows, preferred_element_type=jnp.float32
    )
    mixed_low = mixed_rows.astype(jnp.bfloat16).reshape(token_count, feature_width)
    hidden = (
        residual + jnp.dot(mixed_low, out_weight, preferred_element_type=jnp.float32) + out_shift
    )
    normed_mid, hat_two, inverse_two = layer_norm(hidden, gain_two, shift_two)
    route_prob = jax.nn.softmax(jnp.dot(normed_mid, router_weight, precision=highest), axis=1)
    picked = (
        route_ids[:, :, None] == lax.broadcasted_iota(jnp.int32, (1, 1, expert_total), 2)
    ).astype(jnp.int32)
    picked_float = picked.astype(jnp.float32)
    gate_values = jnp.sum(picked_float * route_prob[:, None, :], axis=2)
    picked_flat = picked.reshape(token_count * route_top, expert_total)
    slot_rank = jnp.sum(
        (jnp.cumsum(picked_flat, axis=0, dtype=jnp.int32) - picked_flat) * picked_flat,
        axis=1,
        dtype=jnp.int32,
    )
    slot_index = route_ids.reshape(-1) * capacity + slot_rank
    mid_low = normed_mid.astype(jnp.bfloat16)
    slot_rows = jnp.broadcast_to(
        mid_low[:, None, :], (token_count, route_top, feature_width)
    ).reshape(token_count * route_top, feature_width)
    outgoing = (
        jnp.zeros((expert_total * capacity, feature_width), jnp.bfloat16)
        .at[slot_index]
        .set(slot_rows)
        .reshape(expert_total, capacity, feature_width)
    )
    arrived = lax.all_to_all(outgoing, "expert", split_axis=0, concat_axis=0, tiled=True)
    flat_in = arrived.reshape(-1, feature_width)
    activation = gelu_exact(
        jnp.dot(flat_in, first_weight, preferred_element_type=jnp.float32) + first_bias
    ).astype(jnp.bfloat16)
    result = (
        jnp.dot(activation, second_weight, preferred_element_type=jnp.float32) + second_bias
    ).astype(jnp.bfloat16)
    produced = result.reshape(arrived.shape)
    returned = lax.all_to_all(produced, "expert", split_axis=0, concat_axis=0, tiled=True)
    slot_out = (
        returned.reshape(expert_total * capacity, feature_width)[slot_index]
        .astype(jnp.float32)
        .reshape(token_count, route_top, feature_width)
    )
    output = (
        (hidden + jnp.sum(gate_values[:, :, None] * slot_out, axis=1))
        .astype(jnp.bfloat16)
        .reshape(tokens.shape)
    )
    upstream = grad_output.astype(jnp.float32).reshape(token_count, feature_width)
    gate_grad = jnp.sum(slot_out * upstream[:, None, :], axis=2)
    slot_grad = (
        (gate_values[:, :, None] * upstream[:, None, :])
        .astype(jnp.bfloat16)
        .reshape(token_count * route_top, feature_width)
    )
    grad_buffer = (
        jnp.zeros((expert_total * capacity, feature_width), jnp.bfloat16)
        .at[slot_index]
        .set(slot_grad)
        .reshape(expert_total, capacity, feature_width)
    )
    grad_arrived = lax.all_to_all(grad_buffer, "expert", split_axis=0, concat_axis=0, tiled=True)
    flat_rows = arrived.reshape(-1, feature_width)
    flat_grad = grad_arrived.reshape(-1, feature_width)
    activation, gelu_back = jax.vjp(
        gelu_exact,
        jnp.dot(flat_rows, first_weight, preferred_element_type=jnp.float32) + first_bias,
    )
    act_low = activation.astype(jnp.bfloat16)
    grad_second = jnp.einsum("rh,rd->hd", act_low, flat_grad, preferred_element_type=jnp.float32)
    grad_second_bias = jnp.sum(flat_grad, axis=0, dtype=jnp.float32)
    act_grad = jnp.einsum("rd,hd->rh", flat_grad, second_weight, preferred_element_type=jnp.float32)
    pre_grad = gelu_back(act_grad)[0].astype(jnp.bfloat16)
    grad_first = jnp.einsum("rd,rh->dh", flat_rows, pre_grad, preferred_element_type=jnp.float32)
    grad_first_bias = jnp.sum(pre_grad, axis=0, dtype=jnp.float32)
    row_grad = (
        jnp.einsum("rh,dh->rd", pre_grad, first_weight, preferred_element_type=jnp.float32)
        .astype(jnp.bfloat16)
        .reshape(grad_arrived.shape)
    )
    row_back = lax.all_to_all(row_grad, "expert", split_axis=0, concat_axis=0, tiled=True)
    slot_back = (
        row_back.reshape(expert_total * capacity, feature_width)[slot_index]
        .astype(jnp.float32)
        .reshape(token_count, route_top, feature_width)
    )
    prob_grad = jnp.sum(picked_float * gate_grad[:, :, None], axis=1)
    logit_grad = route_prob * (prob_grad - jnp.sum(route_prob * prob_grad, axis=1, keepdims=True))
    mid_grad = jnp.sum(slot_back, axis=1) + jnp.einsum(
        "re,de->rd", logit_grad, router_weight, precision=highest
    )
    grad_router = jnp.einsum("rd,re->de", normed_mid, logit_grad, precision=highest)
    norm_part, grad_gain_two, grad_shift_two = norm_backward(
        mid_grad, gain_two, hat_two, inverse_two
    )
    hidden_grad = upstream + norm_part
    branch_low = hidden_grad.astype(jnp.bfloat16)
    grad_out_weight = jnp.einsum(
        "rd,re->de", mixed_low, branch_low, preferred_element_type=jnp.float32
    )
    grad_out_shift = jnp.sum(branch_low, axis=0, dtype=jnp.float32)
    mixed_grad = (
        jnp.einsum("re,de->rd", branch_low, out_weight, preferred_element_type=jnp.float32)
        .astype(jnp.bfloat16)
        .reshape(head_shape)
    )
    score_again = (
        jnp.einsum("bqhd,bkhd->bhqk", queries, key_rows, preferred_element_type=jnp.float32)
        * score_scale
    )
    attn_prob = jnp.exp(score_again - log_total)
    value_grad = jnp.einsum(
        "bhqk,bqhd->bkhd",
        attn_prob.astype(jnp.bfloat16),
        mixed_grad,
        preferred_element_type=jnp.float32,
    ).astype(jnp.bfloat16)
    weight_grad = jnp.einsum(
        "bqhd,bkhd->bhqk", mixed_grad, value_rows, preferred_element_type=jnp.float32
    )
    score_grad = (
        attn_prob * (weight_grad - jnp.sum(attn_prob * weight_grad, axis=3, keepdims=True))
    ).astype(jnp.bfloat16)
    query_grad = (
        jnp.einsum("bhqk,bkhd->bqhd", score_grad, key_rows, preferred_element_type=jnp.float32)
        * score_scale
    ).astype(jnp.bfloat16)
    key_grad = (
        jnp.einsum("bhqk,bqhd->bkhd", score_grad, queries, preferred_element_type=jnp.float32)
        * score_scale
    ).astype(jnp.bfloat16)
    qkv_grad = jnp.concatenate(
        [
            query_grad.reshape(token_count, feature_width),
            key_grad.reshape(token_count, feature_width),
            value_grad.reshape(token_count, feature_width),
        ],
        axis=1,
    )
    grad_qkv = jnp.einsum("rd,re->de", normed_low, qkv_grad, preferred_element_type=jnp.float32)
    grad_query_bias = jnp.sum(qkv_grad[:, :feature_width], axis=0, dtype=jnp.float32)
    grad_value_bias = jnp.sum(qkv_grad[:, 2 * feature_width :], axis=0, dtype=jnp.float32)
    in_grad = jnp.einsum("re,de->rd", qkv_grad, qkv_weight, preferred_element_type=jnp.float32)
    input_part, grad_gain_one, grad_shift_one = norm_backward(
        in_grad, gain_one, hat_one, inverse_one
    )
    input_grad = (hidden_grad + input_part).reshape(tokens.shape)
    shares = (
        lax.psum_scatter(
            grad_gain_one.astype(jnp.bfloat16), "fsdp", scatter_dimension=0, tiled=True
        ).astype(jnp.float32),
        lax.psum_scatter(
            grad_shift_one.astype(jnp.bfloat16), "fsdp", scatter_dimension=0, tiled=True
        ).astype(jnp.float32),
        lax.psum_scatter(
            grad_qkv.astype(jnp.bfloat16), "fsdp", scatter_dimension=0, tiled=True
        ).astype(jnp.float32),
        lax.psum_scatter(
            grad_query_bias.astype(jnp.bfloat16), "fsdp", scatter_dimension=0, tiled=True
        ).astype(jnp.float32),
        lax.psum_scatter(
            grad_value_bias.astype(jnp.bfloat16), "fsdp", scatter_dimension=0, tiled=True
        ).astype(jnp.float32),
        lax.psum_scatter(
            grad_out_weight.astype(jnp.bfloat16), "fsdp", scatter_dimension=0, tiled=True
        ).astype(jnp.float32),
        lax.psum_scatter(
            grad_out_shift.astype(jnp.bfloat16), "fsdp", scatter_dimension=0, tiled=True
        ).astype(jnp.float32),
        lax.psum_scatter(
            grad_gain_two.astype(jnp.bfloat16), "fsdp", scatter_dimension=0, tiled=True
        ).astype(jnp.float32),
        lax.psum_scatter(
            grad_shift_two.astype(jnp.bfloat16), "fsdp", scatter_dimension=0, tiled=True
        ).astype(jnp.float32),
        lax.psum_scatter(
            grad_router.astype(jnp.bfloat16), "fsdp", scatter_dimension=0, tiled=True
        ).astype(jnp.float32),
    )
    summed = (
        lax.psum(shares[0].astype(jnp.bfloat16), "expert").astype(jnp.float32),
        lax.psum(shares[1].astype(jnp.bfloat16), "expert").astype(jnp.float32),
        lax.psum(shares[2].astype(jnp.bfloat16), "expert").astype(jnp.float32),
        lax.psum(shares[3].astype(jnp.bfloat16), "expert").astype(jnp.float32),
        lax.psum(shares[4].astype(jnp.bfloat16), "expert").astype(jnp.float32),
        lax.psum(shares[5].astype(jnp.bfloat16), "expert").astype(jnp.float32),
        lax.psum(shares[6].astype(jnp.bfloat16), "expert").astype(jnp.float32),
        lax.psum(shares[7].astype(jnp.bfloat16), "expert").astype(jnp.float32),
        lax.psum(shares[8].astype(jnp.bfloat16), "expert").astype(jnp.float32),
        lax.psum(shares[9].astype(jnp.bfloat16), "expert").astype(jnp.float32),
    )
    expert_summed = (
        lax.psum_scatter(
            grad_first[None].astype(jnp.bfloat16), "fsdp", scatter_dimension=1, tiled=True
        ).astype(jnp.float32),
        lax.psum_scatter(
            grad_first_bias[None].astype(jnp.bfloat16), "fsdp", scatter_dimension=1, tiled=True
        ).astype(jnp.float32),
        lax.psum_scatter(
            grad_second[None].astype(jnp.bfloat16), "fsdp", scatter_dimension=1, tiled=True
        ).astype(jnp.float32),
        lax.psum_scatter(
            grad_second_bias[None].astype(jnp.bfloat16), "fsdp", scatter_dimension=1, tiled=True
        ).astype(jnp.float32),
    )
    peak_logit = lax.pmax(head_peak, ("expert", "fsdp"))
    limit_value = clip_threshold.astype(jnp.float32)
    root_factor = jnp.sqrt(limit_value / jnp.maximum(peak_logit, limit_value))
    column_scale = jnp.concatenate(
        [
            jnp.repeat(root_factor, head_size),
            jnp.repeat(root_factor, head_size),
            jnp.ones((feature_width,), jnp.float32),
        ]
    )
    clipped_qkv = (w_qkv.astype(jnp.float32) * column_scale).astype(jnp.bfloat16)
    return (
        output,
        input_grad,
        summed[0],
        summed[1],
        summed[2],
        summed[3],
        summed[4],
        summed[5],
        summed[6],
        summed[7],
        summed[8],
        summed[9],
        expert_summed[0],
        expert_summed[1],
        expert_summed[2],
        expert_summed[3],
        clipped_qkv,
    )


def solution(mesh):
    placed = (
        P(("expert", "fsdp"), None, None),
        P("fsdp"),
        P("fsdp"),
        P("fsdp", None),
        P("fsdp"),
        P("fsdp"),
        P("fsdp", None),
        P("fsdp"),
        P("fsdp"),
        P("fsdp"),
        P("fsdp", None),
        P("expert", "fsdp", None),
        P("expert", "fsdp"),
        P("expert", "fsdp", None),
        P("expert", "fsdp"),
        P(("expert", "fsdp"), None),
        P(),
        P(("expert", "fsdp"), None, None),
    )
    return jax.shard_map(
        shards,
        mesh=mesh,
        in_specs=placed,
        out_specs=(
            P(("expert", "fsdp"), None, None),
            P(("expert", "fsdp"), None, None),
            P("fsdp"),
            P("fsdp"),
            P("fsdp", None),
            P("fsdp"),
            P("fsdp"),
            P("fsdp", None),
            P("fsdp"),
            P("fsdp"),
            P("fsdp"),
            P("fsdp", None),
            P("expert", "fsdp", None),
            P("expert", "fsdp"),
            P("expert", "fsdp", None),
            P("expert", "fsdp"),
            P("fsdp", None),
        ),
        check_vma=False,
    )
```

profile of v0, /device:TPU:0, one launch (start us, length us, event | category | flops | bytes accessed | tf_op | source)
XLA Modules:
  0.0 718.8 jit_solution(18381751544721613083)
XLA Ops:
  11.8 6.0 all-gather
  17.8 5.3 all-gather.1
  23.1 5.0 all-gather.2
  28.2 5.0 all-gather.3
  33.2 5.0 all-gather.4
  38.2 5.0 all-gather.5
  43.3 5.0 all-gather.6
  52.3 7.9 %all_gather.47 = bf16[512,512]{1,0:T(8,128)(2,1)} all-gather(bf16[128,512]{1,0:T(8,128)(2,1)S(1)} %copy-done.46), channel_id=1, replica_groups=mesh['expert'=8,'fsdp'=4] {'fsdp'}, dimensions={0}, use_global_device_ids=true | all-gather | bytes 655360 | tf_op jit(solution)/shard_map/all_gather | solution.py:58
  60.2 3.2 fusion.44
  68.6 3.4 copy.109
  74.4 3.1 copy.110
  85.4 5.5 fusion.26
  90.9 2.7 copy.113
  93.5 3.1 reshape.282
  96.7 2.9 fusion.46
  102.7 5.6 reshape.330
  108.3 13.3 %scatter_custom_fusion = bf16[3456,512]{1,0:T(8,128)(2,1)} fusion(s32[1970]{0:T(1024)S(1)} %bitcast.131, bf16[1970,512]{1,0:T(8,128)(2,1)} %reshape.330, bf16[]{:T(256)} %constant.17.clone.1), kind=kCustom, calls=%fused_computation.69 | custom fusion | bytes 3539456 | tf_op jit(solution)/shard_map/scatter | solution.py:138
  121.6 6.0 all-to-all-start
  130.6 4.8 mul.251
  135.5 6.1 mul.252
  141.6 5.2 all_gather.53
  146.8 5.0 all_gather.55
  152.4 5.6 all_gather.51
  161.2 18.5 %scatter_custom_fusion.1 = bf16[3456,512]{1,0:T(8,128)(2,1)} fusion(s32[1970]{0:T(1024)S(1)} %bitcast.132, f32[1970,512]{1,0:T(8,128)} %mul.252, f32[1970]{0:T(1024)S(1)} %mul.249, bf16[]{:T(256)} %constant.17.clone.1), kind=kCustom, calls=%fused_computation.63 | custom fusion | flops 2017280 | bytes 7581698 | tf_op jit(solution)/shard_map/scatter | solution.py:171
  179.8 27.6 %all-to-all-done = bf16[8,432,512]{2,1,0:T(8,128)(2,1)} async-done(((bf16[8,432,512]{2,1,0:T(8,128)(2,1)}), bf16[8,432,512]{2,1,0:T(8,128)(2,1)}, u32[]{:S(2)}, u32[]{:S(2)}) %all-to-all-start) | async-done | bytes 3538976 | tf_op jit(solution)/shard_map/all_to_all | solution.py:141
  207.3 4.7 all-to-all-start.2
  212.0 70.8 %multiply_convert_fusion = (bf16[3456,2048]{1,0:T(8,128)(2,1)}, f32[3456,2048]{1,0:T(8,128)}, f32[3456,2048]{1,0:T(8,128)}) fusion(f32[2048]{0:T(1024)S(1)} %bitcast.142, bf16[3456,512]{1,0:T(8,128)(2,1)} %bitcast.19, bf16[1,512,2048]{2,1,0:T(8,128)(2,1)} %all-gather.13.cloned.1.call-done), kind=kOutput, calls=%fused_computation.7 | convolution fusion | flops 7714897920 | bytes 76423168 | tf_op jit(solution)/shard_map/dot_general | solution.py:144
  282.8 12.5 %add_convert_fusion.1 = bf16[3456,512]{1,0:T(8,128)(2,1)} fusion(bf16[3456,2048]{1,0:T(8,128)(2,1)} %get-tuple-element.48, f32[512]{0:T(512)S(1)} %bitcast.144, bf16[1,2048,512]{2,1,0:T(8,128)(2,1)} %all-gather.15.cloned.1.call-done), kind=kOutput, calls=%fused_computation.25 | convolution fusion | flops 7251296256 | bytes 19793920 | tf_op jit(solution)/shard_map/dot_general | solution.py:147
  295.4 6.0 all-to-all-start.1
  305.0 31.9 %fusion.50 = (bf16[2048]{0:T(1024)(128)(2,1)S(1)}, bf16[3456,2048]{1,0:T(8,128)(2,1)}) fusion(f32[3456,2048]{1,0:T(8,128)} %get-tuple-element.49, bf16[3456,512]{1,0:T(8,128)(2,1)} %bitcast.27, bf16[1,2048,512]{2,1,0:T(8,128)(2,1)} %all-gather.15.cloned.1.call-done, f32[3456,2048]{1,0:T(8,128)} %get-tuple-element.57, f32[2048]{0:T(1024)S(1)} %bitcast.143), kind=kOutput, calls=%fused_computation.138 | convolution fusion | flops 7361001472 | bytes 76427264 | tf_op jit(solution)/shard_map/rd,hd->rh/dot_general | solution.py:184
  338.1 12.6 %convolution_convert_fusion = bf16[3456,512]{1,0:T(8,128)(2,1)} fusion(bf16[3456,2048]{1,0:T(8,128)(2,1)} %get-tuple-element.68, bf16[1,512,2048]{2,1,0:T(8,128)(2,1)} %all-gather.13.cloned.1.call-done), kind=kOutput, calls=%fused_computation.28 | convolution fusion | flops 7249526784 | bytes 19791872 | tf_op jit(solution)/shard_map/rh,dh->rd/dot_general | solution.py:189
  350.7 28.8 %all-to-all-done.1 = bf16[8,432,512]{2,1,0:T(8,128)(2,1)S(1)} async-done(((bf16[8,432,512]{2,1,0:T(8,128)(2,1)}), bf16[8,432,512]{2,1,0:T(8,128)(2,1)S(1)}, u32[]{:S(2)}, u32[]{:S(2)}) %all-to-all-start.1) | async-done | bytes 3538976 | tf_op jit(solution)/shard_map/all_to_all | solution.py:150
  379.6 4.5 all-to-all-start.3
  384.1 13.0 %fusion.7 = bf16[1,2048,512]{2,1,0:T(8,128)(2,1)} fusion(bf16[3456,2048]{1,0:T(8,128)(2,1)} %get-tuple-element.48, bf16[3456,512]{1,0:T(8,128)(2,1)} %bitcast.27), kind=kOutput, calls=%fused_computation.36 | convolution fusion | flops 7248805888 | bytes 19791872 | tf_op jit(solution)/shard_map/rh,rd->hd/dot_general | solution.py:182
  397.7 13.0 %fusion.8 = bf16[1,512,2048]{2,1,0:T(8,128)(2,1)} fusion(bf16[3456,512]{1,0:T(8,128)(2,1)} %bitcast.19, bf16[3456,2048]{1,0:T(8,128)(2,1)} %get-tuple-element.68), kind=kOutput, calls=%fused_computation.37 | convolution fusion | flops 7248805888 | bytes 19791872 | tf_op jit(solution)/shard_map/rd,rh->dh/dot_general | solution.py:186
  410.7 9.1 %gather_fusion = bf16[1970,512]{1,0:T(8,128)(2,1)} fusion(bf16[3456,512]{1,0:T(8,128)(2,1)S(1)} %bitcast.112, s32[2048]{0:T(1024)S(1)} %pad_clamp_fusion), kind=kCustom, calls=%fused_computation | custom fusion | bytes 4042440 | tf_op jit(solution)/shard_map/gather | solution.py:152
  419.9 5.6 reshape.306
  425.5 13.6 %multiply_reduce_fusion.3 = (f32[985,2]{1,0:T(8,128)S(1)}, f32[985,512]{1,0:T(8,128)}) fusion(f32[985,2,512]{2,1,0:T(2,128)} %reshape.306, f32[985,512]{1,0:T(8,128)S(1)} %copy-done.7, f32[985,2]{1,0:T(8,128)S(1)} %copy-done.23), kind=kLoop, calls=%fused_computation.31 | loop fusion | flops 3528270 | bytes 8084880 | tf_op jit(solution)/shard_map/reduce_sum | solution.py:162
  439.4 23.3 %all-to-all-done.3 = bf16[8,432,512]{2,1,0:T(8,128)(2,1)} async-done(((bf16[8,432,512]{2,1,0:T(8,128)(2,1)}), bf16[8,432,512]{2,1,0:T(8,128)(2,1)}, u32[]{:S(2)}, u32[]{:S(2)}) %all-to-all-start.3) | async-done | bytes 3538976 | tf_op jit(solution)/shard_map/all_to_all | solution.py:193
  462.7 10.4 %gather_fusion.1 = bf16[1970,512]{1,0:T(8,128)(2,1)S(1)} fusion(bf16[3456,512]{1,0:T(8,128)(2,1)} %bitcast.29, s32[2048]{0:T(1024)S(1)} %pad_clamp_fusion), kind=kCustom, calls=%fused_computation.1 | custom fusion | bytes 4042440 | tf_op jit(solution)/shard_map/gather | solution.py:195
  473.1 4.7 reshape.309
  477.8 8.4 %reduce_sum.274 = f32[985,512]{1,0:T(8,128)} reduce(f32[985,2,512]{2,1,0:T(2,128)} %reshape.309, f32[]{:T(128)} %constant.40.clone.1), dimensions={1}, to_apply=%region_15.16 | reduce | flops 504320 | bytes 6051844 | tf_op jit(solution)/shard_map/reduce_sum | solution.py:201
  486.3 4.2 multiply_reduce_fusion.6
  495.9 4.2 copy.119
  500.2 3.4 convolution_convert_fusion.7
  503.6 6.7 multiply_reduce_fusion.1
  510.3 4.7 multiply_convert_fusion.1
  517.6 2.9 fusion.49
  520.6 4.3 fusion.48
  524.8 4.1 copy.129
  528.9 4.0 reshape.300
  532.9 4.0 copy.126
  536.9 4.0 reshape.299
  540.8 2.7 copy.123
  543.5 4.0 reshape.298
  552.0 3.3 convolution_convert_fusion.2
  563.9 38.0 %pmax.7 = f32[8]{0:T(128)S(1)} all-reduce(f32[8]{0:T(128)S(1)} %get-tuple-element.17), channel_id=1, replica_groups=mesh['expert'=8,'fsdp'=4] {'expert','fsdp'}, use_global_device_ids=true, to_apply=%region_58.59 | all-reduce | flops 8 | bytes 64 | tf_op jit(solution)/shard_map/pmax | solution.py:318
  604.4 6.5 multiply_reduce_fusion.7
  611.0 3.7 multiply_add_fusion
  615.1 6.4 all-reduce.10
  622.0 3.2 reshape.301
  627.2 4.5 reduce-scatter.22.cloned.1.call-done
  632.5 21.7 %all-reduce.8 = (bf16[128]{0:T(256)(128)(2,1)S(1)}, bf16[128]{0:T(256)(128)(2,1)S(1)}, bf16[128]{0:T(256)(128)(2,1)S(1)}, bf16[128]{0:T(256)(128)(2,1)S(1)}, bf1...) all-reduce(bf16[128]{0:T(256)(128)(2,1)S(1)} %dynamic-slice.1, ...), channel_id=1, replica_groups=mesh['expert'=8,'fsdp'=4] {'expert'}, use_global_device_ids=true, to_apply=%region_26.27 | all-reduce | flops 1920 | bytes 7680 | tf_op jit(solution)/shard_map/psum | solution.py:293
  658.4 49.8 %all-reduce.13.cloned.1.call-done = (bf16[128,1536]{1,0:T(8,128)(2,1)}, bf16[128,512]{1,0:T(8,128)(2,1)}) async-done(((bf16[128,1536]{1,0:T(8,128)(2,1)}, bf16[128,512]{1,0:T(8,128)(2,1)}), (bf16[128,1536]{1,0:T(8,128)(2,1)}, bf16[128,512]{1,0:T(8,128)(2,1)})) %all-reduce.13.cloned.1.call-update) | async-done | bytes 524304 | tf_op jit(solution)/shard_map/psum | solution.py:295
  (294 shorter events, 73.5 us)
Async XLA Ops:
  7.2 10.6 %copy-start.67 = (bf16[128]{0:T(256)(128)(2,1)S(1)}, bf16[128]{0:T(256)(128)(2,1)}, u32[]{:S(2)}) copy-start(bf16[128]{0:T(256)(128)(2,1)} %param.20) | copy-start | bytes 772
  7.2 15.9 %copy-start.68 = (bf16[128]{0:T(256)(128)(2,1)S(1)}, bf16[128]{0:T(256)(128)(2,1)}, u32[]{:S(2)}) copy-start(bf16[128]{0:T(256)(128)(2,1)} %param.23) | copy-start | bytes 772
  7.2 20.9 %copy-start.69 = (bf16[128]{0:T(256)(128)(2,1)S(1)}, bf16[128]{0:T(256)(128)(2,1)}, u32[]{:S(2)}) copy-start(bf16[128]{0:T(256)(128)(2,1)} %param.22) | copy-start | bytes 772
  7.2 25.9 %copy-start.70 = (bf16[128]{0:T(256)(128)(2,1)S(1)}, bf16[128]{0:T(256)(128)(2,1)}, u32[]{:S(2)}) copy-start(bf16[128]{0:T(256)(128)(2,1)} %param.25) | copy-start | bytes 772
  7.3 31.0 %copy-start.71 = (bf16[128]{0:T(256)(128)(2,1)S(1)}, bf16[128]{0:T(256)(128)(2,1)}, u32[]{:S(2)}) copy-start(bf16[128]{0:T(256)(128)(2,1)} %param.26) | copy-start | bytes 772
  7.3 36.0 %copy-start.72 = (bf16[128]{0:T(256)(128)(2,1)S(1)}, bf16[128]{0:T(256)(128)(2,1)}, u32[]{:S(2)}) copy-start(bf16[128]{0:T(256)(128)(2,1)} %param.27) | copy-start | bytes 772
  7.3 41.0 %copy-start.44 = (s32[985,2]{0,1:T(2,128)S(1)}, s32[985,2]{0,1:T(2,128)}, u32[]{:S(2)}) copy-start(s32[985,2]{0,1:T(2,128)} %param.33) | copy-start | bytes 23644
  7.3 53.0 %all-gather.11.cloned.1.call-start = ((), (), s32[]{:S(2)}) async-start(), calls=%async_computation.11 | async-start | bytes 1966080 | tf_op jit(solution)/shard_map/all_gather | solution.py:55
  9.5 42.8 %copy-start.46 = (bf16[128,512]{1,0:T(8,128)(2,1)S(1)}, bf16[128,512]{1,0:T(8,128)(2,1)}, u32[]{:S(2)}) copy-start(bf16[128,512]{1,0:T(8,128)(2,1)} %param.24) | copy-start | bytes 393220
  11.0 52.5 %copy-start.4 = (f32[985,512]{1,0:T(8,128)}, f32[985,512]{1,0:T(8,128)S(1)}, u32[]{:S(2)}) copy-start(f32[985,512]{1,0:T(8,128)S(1)} %reshape.278) | copy-start | bytes 6051844
  11.1 52.4 %copy-start.40 = (f32[985]{0:T(1024)}, f32[985]{0:T(1024)S(1)}, u32[]{:S(2)}) copy-start(f32[985]{0:T(1024)S(1)} %div.38) | copy-start | bytes 11824
  11.8 51.7 %copy-start.42 = (f32[985]{0:T(1024)}, f32[985]{0:T(1024)S(1)}, u32[]{:S(2)}) copy-start(f32[985]{0:T(1024)S(1)} %rsqrt.20) | copy-start | bytes 11824
  17.8 45.7 %copy-start.47 = (f32[4,1,128]{2,1,0:T(1,128)}, f32[4,1,128]{2,1,0:T(1,128)S(1)}, u32[]{:S(2)}) copy-start(f32[4,1,128]{2,1,0:T(1,128)S(1)} %convert_element_type.334) | copy-start | bytes 6148
  23.1 40.4 %copy-start.55 = (f32[4,1,128]{2,1,0:T(1,128)}, f32[4,1,128]{2,1,0:T(1,128)S(1)}, u32[]{:S(2)}) copy-start(f32[4,1,128]{2,1,0:T(1,128)S(1)} %convert_element_type.335) | copy-start | bytes 6148
  43.3 114.8 %copy-start.51 = (f32[4,1,128]{2,1,0:T(1,128)}, f32[4,1,128]{2,1,0:T(1,128)S(1)}, u32[]{:S(2)}) copy-start(f32[4,1,128]{2,1,0:T(1,128)S(1)} %convert_element_type.339) | copy-start | bytes 6148
  48.3 109.7 %copy-start.61 = (f32[4,1,128]{2,1,0:T(1,128)}, f32[4,1,128]{2,1,0:T(1,128)S(1)}, u32[]{:S(2)}) copy-start(f32[4,1,128]{2,1,0:T(1,128)S(1)} %convert_element_type.340) | copy-start | bytes 6148
  60.2 101.0 %copy-start.59 = (s32[1970,1]{0,1:T(1,128)}, s32[1970,1]{0,1:T(1,128)S(1)}, u32[]{:S(2)}) copy-start(s32[1970,1]{0,1:T(1,128)S(1)} %compare_select_fusion) | copy-start | bytes 23644
  99.6 58.5 %copy-start.1 = (f32[985,512]{1,0:T(8,128)}, f32[985,512]{1,0:T(8,128)S(1)}, u32[]{:S(2)}) copy-start(f32[985,512]{1,0:T(8,128)S(1)} %get-tuple-element.56) | copy-start | bytes 6051844
  99.6 58.5 %copy-start.36 = (f32[985]{0:T(1024)}, f32[985]{0:T(1024)S(1)}, u32[]{:S(2)}) copy-start(f32[985]{0:T(1024)S(1)} %broadcast_multiply_fusion.6) | copy-start | bytes 11824
  100.0 58.0 %copy-start.38 = (f32[985]{0:T(1024)}, f32[985]{0:T(1024)S(1)}, u32[]{:S(2)}) copy-start(f32[985]{0:T(1024)S(1)} %add_rsqrt_fusion.1) | copy-start | bytes 11824
  121.6 7.5 %copy-start.31 = (bf16[5,197,512]{2,1,0:T(8,128)(2,1)S(1)}, bf16[5,197,512]{2,1,0:T(8,128)(2,1)}, u32[]{:S(2)}) copy-start(bf16[5,197,512]{2,1,0:T(8,128)(2,1)} %param.35) | copy-start | bytes 3025924
  121.6 85.7 %all-to-all-start = ((bf16[8,432,512]{2,1,0:T(8,128)(2,1)}), bf16[8,432,512]{2,1,0:T(8,128)(2,1)}, u32[]{:S(2)}, u32[]{:S(2)}) async-start(bf16[8,432,512]{2,1,0:T(8,128)(2,1)} %bitcast.113), calls=%async_computation | async-start | bytes 7077888 | tf_op jit(solution)/shard_map/all_to_all | solution.py:141
  127.6 84.4 %all-gather.13.cloned.1.call-start = ((), (), s32[]{:S(2)}) async-start(), calls=%async_computation.12 | async-start | bytes 2621440 | tf_op jit(solution)/shard_map/all_gather | solution.py:63
  128.3 154.5 %all-gather.15.cloned.1.call-start = ((), (), s32[]{:S(2)}) async-start(), calls=%async_computation.13 | async-start | bytes 2621440 | tf_op jit(solution)/shard_map/all_gather | solution.py:65
  135.4 6.1 copy-start.63
  135.4 11.3 %copy-start.73 = (bf16[1,128]{1,0:T(2,128)(2,1)S(1)}, bf16[1,128]{1,0:T(2,128)(2,1)}, u32[]{:S(2)}) copy-start(bf16[1,128]{1,0:T(2,128)(2,1)} %param.32) | copy-start | bytes 772
  135.5 17.0 %copy-start.64 = (bf16[128,8]{0,1:T(8,128)(2,1)S(1)}, bf16[128,8]{0,1:T(8,128)(2,1)}, u32[]{:S(2)}) copy-start(bf16[128,8]{0,1:T(8,128)(2,1)} %param.28) | copy-start | bytes 6148
  158.0 21.7 %copy-start.49 = (bf16[512,8]{0,1:T(8,128)(2,1)}, bf16[512,8]{0,1:T(8,128)(2,1)S(1)}, u32[]{:S(2)}) copy-start(bf16[512,8]{0,1:T(8,128)(2,1)S(1)} %all_gather.51) | copy-start | bytes 24580
  159.5 20.3 %copy-start.53 = (f32[985]{0:T(1024)}, f32[985]{0:T(1024)S(1)}, u32[]{:S(2)}) copy-start(f32[985]{0:T(1024)S(1)} %get-tuple-element.58) | copy-start | bytes 11824
  159.5 20.2 %copy-start.57 = (f32[985]{0:T(1024)}, f32[985]{0:T(1024)S(1)}, u32[]{:S(2)}) copy-start(f32[985]{0:T(1024)S(1)} %fusion.38) | copy-start | bytes 11824
  160.9 18.8 %copy-start.22 = (f32[985,2]{1,0:T(8,128)}, f32[985,2]{1,0:T(8,128)S(1)}, u32[]{:S(2)}) copy-start(f32[985,2]{1,0:T(8,128)S(1)} %copy.114) | copy-start | bytes 23644
  207.3 88.1 %all-to-all-start.2 = ((bf16[8,432,512]{2,1,0:T(8,128)(2,1)}), bf16[8,432,512]{2,1,0:T(8,128)(2,1)}, u32[]{:S(2)}, u32[]{:S(2)}) async-start(bf16[8,432,512]{2,1,0:T(8,128)(2,1)} %bitcast.26), calls=%async_computation.2 | async-start | bytes 7077888 | tf_op jit(solution)/shard_map/all_to_all | solution.py:174
  212.0 70.8 %copy-start.65 = (f32[1,512]{1,0:T(1,128)S(1)}, f32[1,512]{1,0:T(1,128)}, u32[]{:S(2)}) copy-start(f32[1,512]{1,0:T(1,128)} %add.210) | copy-start | bytes 6148
  295.4 84.2 %all-to-all-start.1 = ((bf16[8,432,512]{2,1,0:T(8,128)(2,1)}), bf16[8,432,512]{2,1,0:T(8,128)(2,1)S(1)}, u32[]{:S(2)}, u32[]{:S(2)}) async-start(bf16[8,432,512]{2,1,0:T(8,128)(2,1)} %bitcast.115), calls=%async_computation.1 | async-start | bytes 7077888 | tf_op jit(solution)/shard_map/all_to_all | solution.py:150
  301.4 255.3 %reduce-scatter.26.cloned.1.call-start = ((), (), s32[]{:S(2)}) async-start(), calls=%async_computation.20 | async-start | bytes 163840
  304.8 253.3 %reduce-scatter.24.cloned.1.call-start = ((), (), s32[]{:S(2)}) async-start(), calls=%async_computation.19 | async-start | bytes 655360
  379.6 83.1 %all-to-all-start.3 = ((bf16[8,432,512]{2,1,0:T(8,128)(2,1)}), bf16[8,432,512]{2,1,0:T(8,128)(2,1)}, u32[]{:S(2)}, u32[]{:S(2)}) async-start(bf16[8,432,512]{2,1,0:T(8,128)(2,1)} %bitcast.114), calls=%async_computation.3 | async-start | bytes 7077888 | tf_op jit(solution)/shard_map/all_to_all | solution.py:193
  384.1 13.6 %copy-start.60 = (s32[1970,1]{0,1:T(1,128)S(1)}, s32[1970,1]{0,1:T(1,128)}, u32[]{:S(2)}) copy-start(s32[1970,1]{0,1:T(1,128)} %copy-done.59) | copy-start | bytes 23644
  384.1 175.5 %reduce-scatter.20.cloned.1.call-start = ((), (), s32[]{:S(2)}) async-start(), calls=%async_computation.17 | async-start | bytes 2621440 | tf_op jit(solution)/shard_map/reduce_scatter | solution.py:311
  397.2 164.6 %reduce-scatter.18.cloned.1.call-start = ((), (), s32[]{:S(2)}) async-start(), calls=%async_computation.16 | async-start | bytes 2621440 | tf_op jit(solution)/shard_map/reduce_scatter | solution.py:305
  410.7 204.2 %reduce-scatter.16.cloned.1.call-start = ((), (), s32[]{:S(2)}) async-start(), calls=%async_computation.15 | async-start | bytes 655360 | tf_op jit(solution)/shard_map/reduce_scatter | solution.py:276
  419.9 5.6 copy-start.23
  425.5 13.8 %copy-start.45 = (s32[985,2]{0,1:T(2,128)S(1)}, s32[985,2]{0,1:T(2,128)}, u32[]{:S(2)}) copy-start(s32[985,2]{0,1:T(2,128)} %param.33) | copy-start | bytes 23644
  425.5 13.8 %copy-start.35 = (f32[985,8]{0,1:T(8,128)S(1)}, f32[985,8]{0,1:T(8,128)}, u32[]{:S(2)}) copy-start(f32[985,8]{0,1:T(8,128)} %copy-done.34) | copy-start | bytes 94564
  425.5 13.8 %copy-start.54 = (f32[985]{0:T(1024)S(1)}, f32[985]{0:T(1024)}, u32[]{:S(2)}) copy-start(f32[985]{0:T(1024)} %copy-done.53) | copy-start | bytes 11824
  425.5 13.8 %copy-start.58 = (f32[985]{0:T(1024)S(1)}, f32[985]{0:T(1024)}, u32[]{:S(2)}) copy-start(f32[985]{0:T(1024)} %copy-done.57) | copy-start | bytes 11824
  477.8 8.4 %copy-start.2 = (f32[985,512]{1,0:T(8,128)S(1)}, f32[985,512]{1,0:T(8,128)}, u32[]{:S(2)}) copy-start(f32[985,512]{1,0:T(8,128)} %copy-done.1) | copy-start | bytes 6051844
  477.8 8.4 %copy-start.33 = (f32[985,8]{0,1:T(8,128)S(1)}, f32[985,8]{0,1:T(8,128)}, u32[]{:S(2)}) copy-start(f32[985,8]{0,1:T(8,128)} %copy-done.32) | copy-start | bytes 94564
  477.8 8.4 %copy-start.37 = (f32[985]{0:T(1024)S(1)}, f32[985]{0:T(1024)}, u32[]{:S(2)}) copy-start(f32[985]{0:T(1024)} %copy-done.36) | copy-start | bytes 11824
  477.8 8.4 %copy-start.39 = (f32[985]{0:T(1024)S(1)}, f32[985]{0:T(1024)}, u32[]{:S(2)}) copy-start(f32[985]{0:T(1024)} %copy-done.38) | copy-start | bytes 11824
  477.8 8.4 %copy-start.50 = (bf16[512,8]{0,1:T(8,128)(2,1)S(1)}, bf16[512,8]{0,1:T(8,128)(2,1)}, u32[]{:S(2)}) copy-start(bf16[512,8]{0,1:T(8,128)(2,1)} %copy-done.49) | copy-start | bytes 24580
  477.8 8.4 %copy-start.52 = (f32[4,1,128]{2,1,0:T(1,128)S(1)}, f32[4,1,128]{2,1,0:T(1,128)}, u32[]{:S(2)}) copy-start(f32[4,1,128]{2,1,0:T(1,128)} %copy-done.51) | copy-start | bytes 6148
  495.9 7.7 %copy-start.13 = (bf16[5,197,8,64]{1,3,2,0:T(8,128)(2,1)S(1)}, bf16[5,197,8,64]{1,3,2,0:T(8,128)(2,1)}, u32[]{:S(2)}) copy-start(bf16[5,197,8,64]{1,3,2,0:T(8,128)(2,1)} %copy-done.12) | copy-start | bytes 3025924
  495.9 7.7 %copy-start.30 = (f32[5,8,197]{2,1,0:T(8,128)S(1)}, f32[5,8,197]{2,1,0:T(8,128)}, u32[]{:S(2)}) copy-start(f32[5,8,197]{2,1,0:T(8,128)} %copy-done.29) | copy-start | bytes 94564
  503.6 14.0 %slice-start = ((s8[8192000]{0:T(1024)(128)(4,1)}), s8[4194304]{0:T(1024)(128)(4,1)S(1)}, s32[]{:S(2)}) async-start(s8[8192000]{0:T(1024)(128)(4,1)} %bitcast.110), calls=%async_computation.22 | async-start | bytes 8388608
  510.3 7.3 %slice-start.1 = ((s8[8192000]{0:T(1024)(128)(4,1)}), s8[3997696]{0:T(1024)(128)(4,1)S(1)}, s32[]{:S(2)}) async-start(s8[8192000]{0:T(1024)(128)(4,1)} %bitcast.110), calls=%async_computation.23 | async-start | bytes 7995392
  520.5 94.3 %reduce-scatter.14.cloned.1.call-start = ((), (), s32[]{:S(2)}) async-start(), calls=%async_computation.14 | async-start | bytes 1966080 | tf_op jit(solution)/shard_map/reduce_scatter | solution.py:267
  532.9 7.9 %copy-start.19 = (bf16[5,197,8,64]{1,3,2,0:T(8,128)(2,1)S(1)}, bf16[5,197,8,64]{1,3,2,0:T(8,128)(2,1)}, u32[]{:S(2)}) copy-start(bf16[5,197,8,64]{1,3,2,0:T(8,128)(2,1)} %get-tuple-element.64) | copy-start | bytes 3025924
  543.5 6.8 copy-start.26
  555.3 46.7 %copy-start.62 = (f32[4,1,128]{2,1,0:T(1,128)S(1)}, f32[4,1,128]{2,1,0:T(1,128)}, u32[]{:S(2)}) copy-start(f32[4,1,128]{2,1,0:T(1,128)} %copy-done.61) | copy-start | bytes 6148
  555.3 76.4 %reduce-scatter.22.cloned.1.call-start = ((), (), s32[]{:S(2)}) async-start(), calls=%async_computation.18 | async-start | bytes 163840
  604.4 6.6 copy-start.6
  610.9 97.3 %all-reduce.13.cloned.1.call-start = ((), (), s32[]{:S(2)}) async-start(), calls=%async_computation.21 | async-start | bytes 1048576 | tf_op jit(solution)/shard_map/psum | solution.py:295
  614.7 10.5 %copy-start.24 = (bf16[985,512]{1,0:T(8,128)(2,1)S(1)}, bf16[985,512]{1,0:T(8,128)(2,1)}, u32[]{:S(2)}) copy-start(bf16[985,512]{1,0:T(8,128)(2,1)} %get-tuple-element.52) | copy-start | bytes 3025924
  (29 other events, 100.3 us)
Sparse Core Ops, SparseCore 0:
  9.7 22.3 all-gather.10
  130.0 24.0 all-gather.12
  155.6 22.5 all-gather.14
  304.9 21.0 reduce-scatter.25
  338.2 23.0 reduce-scatter.23
  397.3 32.7 reduce-scatter.19
  432.8 31.4 reduce-scatter.17
  520.6 20.7 reduce-scatter.15
  555.4 27.4 reduce-scatter.13
  611.0 20.5 reduce-scatter.21
  635.5 72.6 all-reduce.12
where the time goes:
time: 726 us; the launch traced here: 719 us
  matrix products  204 us (28%)
  local copies, waits for them, and re-layouts  138 us (19%)
  waiting for transfers between devices  136 us (19%)
  blocking collectives  126 us (17%)
  other arithmetic  76 us (10%)
  starting transfers between devices  22.2 us (3%)
  between operations  16.1 us (2%)
    dot_general x1, matrix products, shards(): jnp.dot(flat_in, first_weight, preferred_element_type=jnp.float32)  70.8 us
    psum x1, waiting for transfers between devices, shards(): lax.psum(shares[2].astype(jnp.bfloat16), 'expert').astype(jnp.float32)  49.8 us
    pmax x1, blocking collectives, shards(): peak_logit = lax.pmax(head_peak, ('expert', 'fsdp'))  38 us
    dot_general x1, matrix products, shards(): jnp.einsum('rd,hd->rh', flat_grad, second_weight, preferred_element_type=...  31.9 us
    all_to_all x1, waiting for transfers between devices, shards(): lax.all_to_all(produced, 'expert', split_axis=0, concat_axis=0, tiled=True)  28.8 us
    all_to_all x1, waiting for transfers between devices, shards(): lax.all_to_all(outgoing, 'expert', split_axis=0, concat_axis=0, tiled=True)  27.6 us
    all_to_all x1, waiting for transfers between devices, shards(): lax.all_to_all(row_grad, 'expert', split_axis=0, concat_axis=0, tiled=True)  23.3 us
    psum x1, blocking collectives, shards(): lax.psum(shares[0].astype(jnp.bfloat16), 'expert').astype(jnp.float32)  21.7 us
  transfers between devices with their start and end apart: 15, of which 5 were waited for; matrix products, arithmetic and copies ran while one was open for 49% of the time, Pallas kernels for 0%

commit v1 on v0

--- a/solution.py
+++ b/solution.py
@@ -6,6 +6,28 @@
 HEADS = 8
 norm_eps = 1e-06
 highest = lax.Precision.HIGHEST
+
+
+def split_up(array, dim, size):
+    before, after = (array.shape[:dim], array.shape[dim + 1 :])
+    return jnp.moveaxis(array.reshape(*before, size, -1, *after), dim, 0)
+
+
+def in_order(blocks, dim):
+    blocks = jnp.moveaxis(blocks, 0, dim)
+    lengths = blocks.shape
+    return blocks.reshape(*lengths[:dim], lengths[dim] * lengths[dim + 1], *lengths[dim + 2 :])
+
+
+def exchange_in_pairs(value, axis, split_dim, concat_dim):
+    length, index = (lax.axis_size(axis), lax.axis_index(axis))
+    pieces = split_up(value, split_dim, length)
+    outs = [pieces[index]]
+    for step in range(1, length):
+        sent = pieces[index ^ step]
+        outs.append(lax.ppermute(sent, axis, [(i, i ^ step) for i in range(length)]))
+    pieces = jnp.stack(outs)[index ^ jnp.arange(length)]
+    return in_order(pieces, concat_dim)
 
 
 def layer_norm(matrix, norm_gain, norm_shift):
@@ -138,7 +160,7 @@
         .set(slot_rows)
         .reshape(expert_total, capacity, feature_width)
     )
-    arrived = lax.all_to_all(outgoing, "expert", split_axis=0, concat_axis=0, tiled=True)
+    arrived = exchange_in_pairs(outgoing, "expert", 0, 0)
     flat_in = arrived.reshape(-1, feature_width)
     activation = gelu_exact(
         jnp.dot(flat_in, first_weight, preferred_element_type=jnp.float32) + first_bias

time: 726 us -> 839 us (1.16)
  waiting for transfers between devices: 136 us -> 227 us
  local copies, waits for them, and re-layouts: 138 us -> 152 us
  starting transfers between devices: 22.2 us -> 32.4 us
    ppermute x0 -> x7, waiting for transfers between devices: none -> 143 us  [exchange_in_pairs(): lax.ppermute(sent, axis, [(i, i ^ step) for i in range(length)])]
    all_to_all x1 -> x0, waiting for transfers between devices: 27.6 us -> none  [shards(): lax.all_to_all(outgoing, 'expert', split_axis=0, concat_axis=0, tiled=True)]
    ppermute x0 -> x7, starting transfers between devices: none -> 13.1 us  [exchange_in_pairs(): lax.ppermute(sent, axis, [(i, i ^ step) for i in range(length)])]
    psum x1, waiting for transfers between devices: 49.8 us -> 38.5 us  [shards(): lax.psum(shares[2].astype(jnp.bfloat16), 'expert').astype(jnp.float32)]
    all_to_all x1, waiting for transfers between devices: 23.3 us -> 13.5 us  [shards(): lax.all_to_all(row_grad, 'expert', split_axis=0, concat_axis=0, tiled=True)]
    unnamed x175 -> x183, local copies, waits for them, and re-layouts: 15.2 us -> 23.6 us
  transfers between devices with their start and end apart: 15 -> 21, of which waited for: 5 -> 6; matrix products, arithmetic and copies ran while one was open for 49% -> 50% of each run, Pallas kernels for 0% -> 0%
where the time goes in v1:
time: 839 us; the launch traced here: 833 us
  waiting for transfers between devices  227 us (27%)
  matrix products  201 us (24%)
  local copies, waits for them, and re-layouts  152 us (18%)
  blocking collectives  126 us (15%)
  other arithmetic  78.4 us (9%)
  starting transfers between devices  32.4 us (4%)
  between operations  15.9 us (2%)
    ppermute x7, waiting for transfers between devices, exchange_in_pairs(): lax.ppermute(sent, axis, [(i, i ^ step) for i in range(length)])  143 us
    dot_general x1, matrix products, shards(): jnp.dot(flat_in, first_weight, preferred_element_type=jnp.float32)  70.8 us
    psum x1, waiting for transfers between devices, shards(): lax.psum(shares[2].astype(jnp.bfloat16), 'expert').astype(jnp.float32)  38.5 us
    pmax x1, blocking collectives, shards(): peak_logit = lax.pmax(head_peak, ('expert', 'fsdp'))  37.2 us
    dot_general x1, matrix products, shards(): jnp.einsum('rd,hd->rh', flat_grad, second_weight, preferred_element_type=...  32.2 us
    all_to_all x1, waiting for transfers between devices, shards(): lax.all_to_all(produced, 'expert', split_axis=0, concat_axis=0, tiled=True)  29.8 us
    unnamed x183, local copies, waits for them, and re-layouts  23.6 us
    psum x1, blocking collectives, shards(): lax.psum(shares[0].astype(jnp.bfloat16), 'expert').astype(jnp.float32)  20.5 us
  transfers between devices with their start and end apart: 21, of which 6 were waited for; matrix products, arithmetic and copies ran while one was open for 50% of the time, Pallas kernels for 0%

profile of v1, /device:TPU:0, one launch (start us, length us, event | category | flops | bytes accessed | tf_op | source)
XLA Modules:
  0.0 833.4 jit_solution(1059390300763560085)
XLA Ops:
  14.2 6.0 all-gather
  20.2 5.3 all-gather.1
  25.5 5.0 all-gather.3
  30.6 5.0 all-gather.2
  35.6 5.0 all-gather.4
  40.6 5.0 all-gather.5
  45.7 5.0 all-gather.6
  50.7 5.0 all_gather.55
  56.4 5.2 all_gather.51
  61.5 5.2 all_gather.53
  72.8 10.3 %all_gather.47 = bf16[512,512]{1,0:T(8,128)(2,1)} all-gather(bf16[128,512]{1,0:T(8,128)(2,1)S(1)} %copy-done.46), channel_id=1, replica_groups=mesh['expert'=8,'fsdp'=4] {'fsdp'}, dimensions={0}, use_global_device_ids=true | all-gather | bytes 655360 | tf_op jit(solution)/shard_map/all_gather | solution.py:80
  83.1 2.8 reshape.315
  85.9 4.9 mul.251
  90.7 5.9 mul.252
  96.6 3.2 fusion.45
  104.9 4.0 copy.109
  111.3 3.1 copy.110
  114.4 4.1 reshape.288
  118.5 4.1 copy.111
  130.8 2.7 copy.113
  133.5 3.1 reshape.291
  145.2 12.5 %scatter_custom_fusion = bf16[3456,512]{1,0:T(8,128)(2,1)S(1)} fusion(s32[1970]{0:T(1024)} %bitcast.169, bf16[1970,512]{1,0:T(8,128)(2,1)} %reshape.347, bf16[]{:T(256)} %constant.55.clone.1), kind=kCustom, calls=%fused_computation.70 | custom fusion | bytes 3539456 | tf_op jit(solution)/shard_map/scatter | solution.py:160
  164.2 18.4 %scatter_custom_fusion.1 = bf16[3456,512]{1,0:T(8,128)(2,1)} fusion(s32[1970]{0:T(1024)} %bitcast.170, f32[1970,512]{1,0:T(8,128)} %mul.252, f32[1970]{0:T(1024)S(1)} %mul.249, bf16[]{:T(256)} %constant.55.clone.1), kind=kCustom, calls=%fused_computation.64 | custom fusion | flops 2017280 | bytes 7594184 | tf_op jit(solution)/shard_map/scatter | solution.py:193
  182.7 4.9 all-to-all-start.1
  187.6 4.8 collective-permute-start.6
  193.5 4.2 collective-permute-start.2
  199.8 86.1 %collective-permute-done.2 = bf16[1,432,512]{2,1,0:T(8,128)(2,1)S(1)} collective-permute-done((bf16[1,432,512]{2,1,0:T(8,128)(2,1)}, bf16[1,432,512]{2,1,0:T(8,128)(2,1)S(1)}, u32[]{:S(2)}, u32[]{:S(2)}) %collective-permute-start.2) | collective-permute-done | bytes 442400 | tf_op jit(solution)/shard_map/ppermute | solution.py:28
  285.9 56.8 %collective-permute-done.3 = bf16[1,432,512]{2,1,0:T(8,128)(2,1)S(1)} collective-permute-done((bf16[1,432,512]{2,1,0:T(8,128)(2,1)}, bf16[1,432,512]{2,1,0:T(8,128)(2,1)S(1)}, u32[]{:S(2)}, u32[]{:S(2)}) %collective-permute-start.3) | collective-permute-done | bytes 442400 | tf_op jit(solution)/shard_map/ppermute | solution.py:28
  345.9 70.8 %multiply_convert_fusion = (bf16[3456,2048]{1,0:T(8,128)(2,1)}, f32[3456,2048]{1,0:T(8,128)}, f32[3456,2048]{1,0:T(8,128)}) fusion(f32[2048]{0:T(1024)S(1)} %bitcast.179, bf16[3456,512]{1,0:T(8,128)(2,1)} %bitcast.149, bf16[1,512,2048]{2,1,0:T(8,128)(2,1)} %all-gather.13.cloned.1.call-done), kind=kOutput, calls=%fused_computation.8 | convolution fusion | flops 7714897920 | bytes 76423168 | tf_op jit(solution)/shard_map/dot_general | solution.py:166
  416.7 12.5 %add_convert_fusion.1 = bf16[3456,512]{1,0:T(8,128)(2,1)} fusion(bf16[3456,2048]{1,0:T(8,128)(2,1)} %get-tuple-element.48, f32[512]{0:T(512)S(1)} %bitcast.181, bf16[1,2048,512]{2,1,0:T(8,128)(2,1)} %all-gather.15.cloned.1.call-done), kind=kOutput, calls=%fused_computation.26 | convolution fusion | flops 7251296256 | bytes 19793920 | tf_op jit(solution)/shard_map/dot_general | solution.py:169
  429.2 10.3 %all-to-all-start = ((bf16[8,432,512]{2,1,0:T(8,128)(2,1)}), bf16[8,432,512]{2,1,0:T(8,128)(2,1)S(1)}, u32[]{:S(2)}, u32[]{:S(2)}) async-start(bf16[8,432,512]{2,1,0:T(8,128)(2,1)} %bitcast.152), calls=%async_computation | async-start | bytes 7077888 | tf_op jit(solution)/shard_map/all_to_all | solution.py:172
  443.0 32.2 %fusion.51 = (bf16[2048]{0:T(1024)(128)(2,1)S(1)}, bf16[3456,2048]{1,0:T(8,128)(2,1)}) fusion(f32[3456,2048]{1,0:T(8,128)} %get-tuple-element.49, bf16[3456,512]{1,0:T(8,128)(2,1)} %bitcast.43, bf16[1,2048,512]{2,1,0:T(8,128)(2,1)} %all-gather.15.cloned.1.call-done, f32[3456,2048]{1,0:T(8,128)} %get-tuple-element.65, f32[2048]{0:T(1024)S(1)} %bitcast.180), kind=kOutput, calls=%fused_computation.157 | convolution fusion | flops 7361001472 | bytes 76427264 | tf_op jit(solution)/shard_map/rd,hd->rh/dot_general | solution.py:206
  476.4 12.7 %convolution_convert_fusion = bf16[3456,512]{1,0:T(8,128)(2,1)} fusion(bf16[3456,2048]{1,0:T(8,128)(2,1)} %get-tuple-element.76, bf16[1,512,2048]{2,1,0:T(8,128)(2,1)} %all-gather.13.cloned.1.call-done), kind=kOutput, calls=%fused_computation.29 | convolution fusion | flops 7249526784 | bytes 19791872 | tf_op jit(solution)/shard_map/rh,dh->rd/dot_general | solution.py:211
  489.0 29.8 %all-to-all-done = bf16[8,432,512]{2,1,0:T(8,128)(2,1)S(1)} async-done(((bf16[8,432,512]{2,1,0:T(8,128)(2,1)}), bf16[8,432,512]{2,1,0:T(8,128)(2,1)S(1)}, u32[]{:S(2)}, u32[]{:S(2)}) %all-to-all-start) | async-done | bytes 3538976 | tf_op jit(solution)/shard_map/all_to_all | solution.py:172
  520.5 3.7 all-to-all-start.2
  524.3 12.1 %gather_fusion.1 = bf16[1970,512]{1,0:T(8,128)(2,1)} fusion(bf16[3456,512]{1,0:T(8,128)(2,1)} %bitcast.146, s32[2048]{0:T(1024)S(1)} %copy-done.51), kind=kCustom, calls=%fused_computation.1 | custom fusion | bytes 4042440 | tf_op jit(solution)/shard_map/gather | solution.py:174
  536.3 5.5 reshape.313
  541.8 13.8 %multiply_reduce_fusion.3 = (f32[985,2]{1,0:T(8,128)}, f32[985,512]{1,0:T(8,128)}) fusion(f32[985,2,512]{2,1,0:T(2,128)} %reshape.313, f32[985,512]{1,0:T(8,128)} %reshape.315, f32[985,2]{1,0:T(8,128)} %copy-done.23), kind=kLoop, calls=%fused_computation.32 | loop fusion | flops 3528270 | bytes 8084880 | tf_op jit(solution)/shard_map/reduce_sum | solution.py:184
  559.6 3.2 fusion.28
  563.7 13.1 %fusion.7 = bf16[1,2048,512]{2,1,0:T(8,128)(2,1)} fusion(bf16[3456,2048]{1,0:T(8,128)(2,1)} %get-tuple-element.48, bf16[3456,512]{1,0:T(8,128)(2,1)} %bitcast.43), kind=kOutput, calls=%fused_computation.37 | convolution fusion | flops 7248805888 | bytes 19791872 | tf_op jit(solution)/shard_map/rh,rd->hd/dot_general | solution.py:204
  576.9 13.0 %fusion.8 = bf16[1,512,2048]{2,1,0:T(8,128)(2,1)} fusion(bf16[3456,512]{1,0:T(8,128)(2,1)} %bitcast.150, bf16[3456,2048]{1,0:T(8,128)(2,1)} %get-tuple-element.76), kind=kOutput, calls=%fused_computation.38 | convolution fusion | flops 7248805888 | bytes 19791872 | tf_op jit(solution)/shard_map/rd,rh->dh/dot_general | solution.py:208
  589.9 13.5 %all-to-all-done.2 = bf16[8,432,512]{2,1,0:T(8,128)(2,1)S(1)} async-done(((bf16[8,432,512]{2,1,0:T(8,128)(2,1)}), bf16[8,432,512]{2,1,0:T(8,128)(2,1)S(1)}, u32[]{:S(2)}, u32[]{:S(2)}) %all-to-all-start.2) | async-done | bytes 3538976 | tf_op jit(solution)/shard_map/all_to_all | solution.py:215
  603.5 9.3 %gather_fusion.2 = bf16[1970,512]{1,0:T(8,128)(2,1)} fusion(bf16[3456,512]{1,0:T(8,128)(2,1)S(1)} %bitcast.145, s32[2048]{0:T(1024)S(1)} %copy-done.52), kind=kCustom, calls=%fused_computation.2 | custom fusion | bytes 4042440 | tf_op jit(solution)/shard_map/gather | solution.py:217
  612.8 5.5 reshape.316
  618.3 8.4 %reduce_sum.274 = f32[985,512]{1,0:T(8,128)} reduce(f32[985,2,512]{2,1,0:T(2,128)} %reshape.316, f32[]{:T(128)} %constant.50.clone.1), dimensions={1}, to_apply=%region_15.16 | reduce | flops 504320 | bytes 6051844 | tf_op jit(solution)/shard_map/reduce_sum | solution.py:223
  626.7 4.8 multiply_reduce_fusion.6
  636.8 4.4 copy.119
  641.2 2.7 convolution_convert_fusion.7
  644.0 6.7 multiply_reduce_fusion.1
  650.7 4.8 multiply_convert_fusion.1
  660.0 2.9 fusion.50
  662.9 3.2 fusion.49
  666.1 4.2 copy.129
  670.4 4.0 reshape.307
  674.3 2.7 copy.126
  677.0 4.0 reshape.306
  681.0 2.7 copy.123
  683.6 4.0 reshape.305
  692.1 3.1 convolution_convert_fusion.2
  704.8 37.2 %pmax.7 = f32[8]{0:T(128)S(1)} all-reduce(f32[8]{0:T(128)S(1)} %get-tuple-element.17), channel_id=1, replica_groups=mesh['expert'=8,'fsdp'=4] {'expert','fsdp'}, use_global_device_ids=true, to_apply=%region_58.59 | all-reduce | flops 8 | bytes 64 | tf_op jit(solution)/shard_map/pmax | solution.py:340
  742.1 4.8 multiply_reduce_fusion.7
  750.6 6.4 all-reduce.10
  757.5 20.5 %all-reduce.8 = (bf16[128]{0:T(256)(128)(2,1)S(1)}, bf16[128]{0:T(256)(128)(2,1)S(1)}, bf16[128]{0:T(256)(128)(2,1)S(1)}, bf16[128]{0:T(256)(128)(2,1)S(1)}, bf1...) all-reduce(bf16[128]{0:T(256)(128)(2,1)S(1)} %dynamic-slice.1, ...), channel_id=1, replica_groups=mesh['expert'=8,'fsdp'=4] {'expert'}, use_global_device_ids=true, to_apply=%region_26.27 | all-reduce | flops 1920 | bytes 7680 | tf_op jit(solution)/shard_map/psum | solution.py:315
  784.6 38.5 %all-reduce.13.cloned.1.call-done = (bf16[128,1536]{1,0:T(8,128)(2,1)}, bf16[128,512]{1,0:T(8,128)(2,1)}) async-done(((bf16[128,1536]{1,0:T(8,128)(2,1)}, bf16[128,512]{1,0:T(8,128)(2,1)}), (bf16[128,1536]{1,0:T(8,128)(2,1)}, bf16[128,512]{1,0:T(8,128)(2,1)})) %all-reduce.13.cloned.1.call-update) | async-done | bytes 524304 | tf_op jit(solution)/shard_map/psum | solution.py:317
  (319 shorter events, 99.3 us)
Async XLA Ops:
  7.2 7.0 copy-start.67
  7.2 12.9 %copy-start.68 = (bf16[128]{0:T(256)(128)(2,1)S(1)}, bf16[128]{0:T(256)(128)(2,1)}, u32[]{:S(2)}) copy-start(bf16[128]{0:T(256)(128)(2,1)} %param.20) | copy-start | bytes 772
  7.2 18.3 %copy-start.69 = (bf16[128]{0:T(256)(128)(2,1)S(1)}, bf16[128]{0:T(256)(128)(2,1)}, u32[]{:S(2)}) copy-start(bf16[128]{0:T(256)(128)(2,1)} %param.22) | copy-start | bytes 772
  7.2 23.3 %copy-start.70 = (bf16[128]{0:T(256)(128)(2,1)S(1)}, bf16[128]{0:T(256)(128)(2,1)}, u32[]{:S(2)}) copy-start(bf16[128]{0:T(256)(128)(2,1)} %param.23) | copy-start | bytes 772
  7.3 28.3 %copy-start.71 = (bf16[128]{0:T(256)(128)(2,1)S(1)}, bf16[128]{0:T(256)(128)(2,1)}, u32[]{:S(2)}) copy-start(bf16[128]{0:T(256)(128)(2,1)} %param.25) | copy-start | bytes 772
  7.3 33.4 %copy-start.72 = (bf16[128]{0:T(256)(128)(2,1)S(1)}, bf16[128]{0:T(256)(128)(2,1)}, u32[]{:S(2)}) copy-start(bf16[128]{0:T(256)(128)(2,1)} %param.26) | copy-start | bytes 772
  7.3 38.4 %copy-start.73 = (bf16[128]{0:T(256)(128)(2,1)S(1)}, bf16[128]{0:T(256)(128)(2,1)}, u32[]{:S(2)}) copy-start(bf16[128]{0:T(256)(128)(2,1)} %param.27) | copy-start | bytes 772
  7.3 43.4 %copy-start.74 = (bf16[1,128]{1,0:T(2,128)(2,1)S(1)}, bf16[1,128]{1,0:T(2,128)(2,1)}, u32[]{:S(2)}) copy-start(bf16[1,128]{1,0:T(2,128)(2,1)} %param.32) | copy-start | bytes 772
  7.3 49.1 %copy-start.64 = (bf16[128,8]{0,1:T(8,128)(2,1)S(1)}, bf16[128,8]{0,1:T(8,128)(2,1)}, u32[]{:S(2)}) copy-start(bf16[128,8]{0,1:T(8,128)(2,1)} %param.28) | copy-start | bytes 6148
  7.3 54.2 %copy-start.65 = (bf16[1,512]{1,0:T(2,128)(2,1)S(1)}, bf16[1,512]{1,0:T(2,128)(2,1)}, u32[]{:S(2)}) copy-start(bf16[1,512]{1,0:T(2,128)(2,1)} %param.30) | copy-start | bytes 3076
  7.3 89.3 %all-gather.11.cloned.1.call-start = ((), (), s32[]{:S(2)}) async-start(), calls=%async_computation.10 | async-start | bytes 1966080 | tf_op jit(solution)/shard_map/all_gather | solution.py:77
  8.1 337.8 %all-gather.13.cloned.1.call-start = ((), (), s32[]{:S(2)}) async-start(), calls=%async_computation.11 | async-start | bytes 2621440 | tf_op jit(solution)/shard_map/all_gather | solution.py:85
  8.8 407.9 %all-gather.15.cloned.1.call-start = ((), (), s32[]{:S(2)}) async-start(), calls=%async_computation.12 | async-start | bytes 2621440 | tf_op jit(solution)/shard_map/all_gather | solution.py:87
  11.1 85.5 %copy-start.40 = (f32[985]{0:T(1024)}, f32[985]{0:T(1024)S(1)}, u32[]{:S(2)}) copy-start(f32[985]{0:T(1024)S(1)} %div.38) | copy-start | bytes 11824
  11.1 61.7 %copy-start.46 = (bf16[128,512]{1,0:T(8,128)(2,1)S(1)}, bf16[128,512]{1,0:T(8,128)(2,1)}, u32[]{:S(2)}) copy-start(bf16[128,512]{1,0:T(8,128)(2,1)} %param.24) | copy-start | bytes 393220
  14.2 122.4 %copy-start.5 = (f32[985,512]{1,0:T(8,128)}, f32[985,512]{1,0:T(8,128)S(1)}, u32[]{:S(2)}) copy-start(f32[985,512]{1,0:T(8,128)S(1)} %reshape.287) | copy-start | bytes 6051844
  20.2 76.5 %copy-start.47 = (f32[4,1,128]{2,1,0:T(1,128)}, f32[4,1,128]{2,1,0:T(1,128)S(1)}, u32[]{:S(2)}) copy-start(f32[4,1,128]{2,1,0:T(1,128)S(1)} %convert_element_type.334) | copy-start | bytes 6148
  25.5 71.1 %copy-start.56 = (f32[4,1,128]{2,1,0:T(1,128)}, f32[4,1,128]{2,1,0:T(1,128)S(1)}, u32[]{:S(2)}) copy-start(f32[4,1,128]{2,1,0:T(1,128)S(1)} %convert_element_type.335) | copy-start | bytes 6148
  45.7 94.0 %copy-start.53 = (f32[4,1,128]{2,1,0:T(1,128)}, f32[4,1,128]{2,1,0:T(1,128)S(1)}, u32[]{:S(2)}) copy-start(f32[4,1,128]{2,1,0:T(1,128)S(1)} %convert_element_type.339) | copy-start | bytes 6148
  50.7 89.0 %copy-start.62 = (f32[4,1,128]{2,1,0:T(1,128)}, f32[4,1,128]{2,1,0:T(1,128)S(1)}, u32[]{:S(2)}) copy-start(f32[4,1,128]{2,1,0:T(1,128)S(1)} %convert_element_type.340) | copy-start | bytes 6148
  61.5 78.2 %copy-start.49 = (bf16[512,8]{0,1:T(8,128)(2,1)}, bf16[512,8]{0,1:T(8,128)(2,1)S(1)}, u32[]{:S(2)}) copy-start(bf16[512,8]{0,1:T(8,128)(2,1)S(1)} %all_gather.51) | copy-start | bytes 24580
  67.4 29.3 %copy-start.42 = (f32[985]{0:T(1024)}, f32[985]{0:T(1024)S(1)}, u32[]{:S(2)}) copy-start(f32[985]{0:T(1024)S(1)} %rsqrt.20) | copy-start | bytes 11824
  72.2 18.5 %copy-start.61 = (s32[1970,1]{0,1:T(1,128)}, s32[1970,1]{0,1:T(1,128)S(1)}, u32[]{:S(2)}) copy-start(s32[1970,1]{0,1:T(1,128)S(1)} %compare_select_fusion) | copy-start | bytes 23644
  114.4 10.8 %copy-start.11 = (bf16[5,197,8,64]{1,3,2,0:T(8,128)(2,1)}, bf16[5,197,8,64]{1,3,2,0:T(8,128)(2,1)S(1)}, u32[]{:S(2)}) copy-start(bf16[5,197,8,64]{1,3,2,0:T(8,128)(2,1)S(1)} %copy.110) | copy-start | bytes 3025924
  142.1 20.4 %copy-start.55 = (f32[985]{0:T(1024)}, f32[985]{0:T(1024)S(1)}, u32[]{:S(2)}) copy-start(f32[985]{0:T(1024)S(1)} %get-tuple-element.66) | copy-start | bytes 11824
  159.5 39.2 %collective-permute-start.1 = (bf16[1,432,512]{2,1,0:T(8,128)(2,1)}, bf16[1,432,512]{2,1,0:T(8,128)(2,1)}, u32[]{:S(2)}, u32[]{:S(2)}) collective-permute-start(bf16[1,432,512]{2,1,0:T(8,128)(2,1)} %get-tuple-element.57), channel_id=1, source_target_pairs={{0,8},{4,12},{8,0},{12,4},{16,24},{20,28},{24,16},{28,20},{1,9},{5... | collective-permute-start | bytes 1327112 | tf_op jit(solution)/shard_map/ppermute | solution.py:28
  161.0 32.5 %collective-permute-start = (bf16[1,432,512]{2,1,0:T(8,128)(2,1)}, bf16[1,432,512]{2,1,0:T(8,128)(2,1)}, u32[]{:S(2)}, u32[]{:S(2)}) collective-permute-start(bf16[1,432,512]{2,1,0:T(8,128)(2,1)} %get-tuple-element.58), channel_id=1, source_target_pairs={{0,4},{4,0},{8,12},{12,8},{16,20},{20,16},{24,28},{28,24},{1,5},{5... | collective-permute-start | bytes 1327112 | tf_op jit(solution)/shard_map/ppermute | solution.py:28
  164.0 18.7 %copy-start.23 = (f32[985,2]{1,0:T(8,128)}, f32[985,2]{1,0:T(8,128)S(1)}, u32[]{:S(2)}) copy-start(f32[985,2]{1,0:T(8,128)S(1)} %copy.114) | copy-start | bytes 23644
  182.7 15.0 %copy-start.24 = (bf16[8,1,432,512]{3,2,0,1:T(8,128)(2,1)S(1)}, bf16[8,1,432,512]{3,2,0,1:T(8,128)(2,1)}, u32[]{:S(2)}) copy-start(bf16[8,1,432,512]{3,2,0,1:T(8,128)(2,1)} %get-tuple-element.59) | copy-start | bytes 10616836
  182.7 246.5 %all-to-all-start.1 = ((bf16[8,432,512]{2,1,0:T(8,128)(2,1)}), bf16[8,432,512]{2,1,0:T(8,128)(2,1)}, u32[]{:S(2)}, u32[]{:S(2)}) async-start(bf16[8,432,512]{2,1,0:T(8,128)(2,1)} %bitcast.42), calls=%async_computation.1 | async-start | bytes 7077888 | tf_op jit(solution)/shard_map/all_to_all | solution.py:196
  187.6 155.7 %collective-permute-start.6 = (bf16[1,432,512]{2,1,0:T(8,128)(2,1)}, bf16[1,432,512]{2,1,0:T(8,128)(2,1)S(1)}, u32[]{:S(2)}, u32[]{:S(2)}) collective-permute-start(bf16[1,432,512]{2,1,0:T(8,128)(2,1)} %get-tuple-element.52), channel_id=1, source_target_pairs={{0,28},{4,24},{8,20},{12,16},{16,12},{20,8},{24,4},{28,0},{1,29},{... | collective-permute-start | bytes 1327112 | tf_op jit(solution)/shard_map/ppermute | solution.py:28
  192.4 150.9 %collective-permute-start.5 = (bf16[1,432,512]{2,1,0:T(8,128)(2,1)}, bf16[1,432,512]{2,1,0:T(8,128)(2,1)S(1)}, u32[]{:S(2)}, u32[]{:S(2)}) collective-permute-start(bf16[1,432,512]{2,1,0:T(8,128)(2,1)} %get-tuple-element.53), channel_id=1, source_target_pairs={{0,24},{4,28},{8,16},{12,20},{16,8},{20,12},{24,0},{28,4},{1,25},{... | collective-permute-start | bytes 1327112 | tf_op jit(solution)/shard_map/ppermute | solution.py:28
  192.9 150.3 %collective-permute-start.4 = (bf16[1,432,512]{2,1,0:T(8,128)(2,1)}, bf16[1,432,512]{2,1,0:T(8,128)(2,1)S(1)}, u32[]{:S(2)}, u32[]{:S(2)}) collective-permute-start(bf16[1,432,512]{2,1,0:T(8,128)(2,1)} %get-tuple-element.54), channel_id=1, source_target_pairs={{0,20},{4,16},{8,28},{12,24},{16,4},{20,0},{24,12},{28,8},{1,21},{... | collective-permute-start | bytes 1327112 | tf_op jit(solution)/shard_map/ppermute | solution.py:28
  193.5 92.4 %collective-permute-start.2 = (bf16[1,432,512]{2,1,0:T(8,128)(2,1)}, bf16[1,432,512]{2,1,0:T(8,128)(2,1)S(1)}, u32[]{:S(2)}, u32[]{:S(2)}) collective-permute-start(bf16[1,432,512]{2,1,0:T(8,128)(2,1)} %get-tuple-element.56), channel_id=1, source_target_pairs={{0,12},{4,8},{8,4},{12,0},{16,28},{20,24},{24,20},{28,16},{1,13},{... | collective-permute-start | bytes 1327112 | tf_op jit(solution)/shard_map/ppermute | solution.py:28
  198.7 144.0 %collective-permute-start.3 = (bf16[1,432,512]{2,1,0:T(8,128)(2,1)}, bf16[1,432,512]{2,1,0:T(8,128)(2,1)S(1)}, u32[]{:S(2)}, u32[]{:S(2)}) collective-permute-start(bf16[1,432,512]{2,1,0:T(8,128)(2,1)} %get-tuple-element.55), channel_id=1, source_target_pairs={{0,16},{4,20},{8,24},{12,28},{16,0},{20,4},{24,8},{28,12},{1,17},{... | collective-permute-start | bytes 1327112 | tf_op jit(solution)/shard_map/ppermute | solution.py:28
  345.9 70.8 %copy-start.66 = (f32[1,512]{1,0:T(1,128)S(1)}, f32[1,512]{1,0:T(1,128)}, u32[]{:S(2)}) copy-start(f32[1,512]{1,0:T(1,128)} %add.253) | copy-start | bytes 6148
  429.2 89.6 %all-to-all-start = ((bf16[8,432,512]{2,1,0:T(8,128)(2,1)}), bf16[8,432,512]{2,1,0:T(8,128)(2,1)S(1)}, u32[]{:S(2)}, u32[]{:S(2)}) async-start(bf16[8,432,512]{2,1,0:T(8,128)(2,1)} %bitcast.152), calls=%async_computation | async-start | bytes 7077888 | tf_op jit(solution)/shard_map/all_to_all | solution.py:172
  439.5 257.1 %reduce-scatter.26.cloned.1.call-start = ((), (), s32[]{:S(2)}) async-start(), calls=%async_computation.19 | async-start | bytes 163840
  442.9 255.0 %reduce-scatter.24.cloned.1.call-start = ((), (), s32[]{:S(2)}) async-start(), calls=%async_computation.18 | async-start | bytes 655360
  520.5 83.0 %all-to-all-start.2 = ((bf16[8,432,512]{2,1,0:T(8,128)(2,1)}), bf16[8,432,512]{2,1,0:T(8,128)(2,1)S(1)}, u32[]{:S(2)}, u32[]{:S(2)}) async-start(bf16[8,432,512]{2,1,0:T(8,128)(2,1)} %bitcast.151), calls=%async_computation.2 | async-start | bytes 7077888 | tf_op jit(solution)/shard_map/all_to_all | solution.py:215
  524.2 175.4 %reduce-scatter.22.cloned.1.call-start = ((), (), s32[]{:S(2)}) async-start(), calls=%async_computation.17 | async-start | bytes 163840
  541.8 15.7 %copy-start.45 = (s32[985,2]{0,1:T(2,128)S(1)}, s32[985,2]{0,1:T(2,128)}, u32[]{:S(2)}) copy-start(s32[985,2]{0,1:T(2,128)} %param.33) | copy-start | bytes 23644
  541.8 17.8 %copy-start.37 = (f32[985]{0:T(1024)S(1)}, f32[985]{0:T(1024)}, u32[]{:S(2)}) copy-start(f32[985]{0:T(1024)} %copy-done.36) | copy-start | bytes 11824
  541.8 17.8 %copy-start.39 = (f32[985]{0:T(1024)S(1)}, f32[985]{0:T(1024)}, u32[]{:S(2)}) copy-start(f32[985]{0:T(1024)} %copy-done.38) | copy-start | bytes 11824
  563.6 136.8 %reduce-scatter.20.cloned.1.call-start = ((), (), s32[]{:S(2)}) async-start(), calls=%async_computation.16 | async-start | bytes 2621440 | tf_op jit(solution)/shard_map/reduce_scatter | solution.py:333
  576.8 26.7 %copy-start.52 = (s32[2048]{0:T(1024)S(1)}, s32[2048]{0:T(1024)}, u32[]{:S(2)}) copy-start(s32[2048]{0:T(1024)} %pad_clamp_fusion) | copy-start | bytes 24580
  576.8 125.8 %reduce-scatter.18.cloned.1.call-start = ((), (), s32[]{:S(2)}) async-start(), calls=%async_computation.15 | async-start | bytes 2621440 | tf_op jit(solution)/shard_map/reduce_scatter | solution.py:327
  589.9 159.2 %reduce-scatter.16.cloned.1.call-start = ((), (), s32[]{:S(2)}) async-start(), calls=%async_computation.14 | async-start | bytes 655360 | tf_op jit(solution)/shard_map/reduce_scatter | solution.py:298
  618.3 8.4 %copy-start.3 = (f32[985,512]{1,0:T(8,128)S(1)}, f32[985,512]{1,0:T(8,128)}, u32[]{:S(2)}) copy-start(f32[985,512]{1,0:T(8,128)} %copy-done.2) | copy-start | bytes 6051844
  618.3 8.4 %copy-start.32 = (f32[985,8]{0,1:T(8,128)S(1)}, f32[985,8]{0,1:T(8,128)}, u32[]{:S(2)}) copy-start(f32[985,8]{0,1:T(8,128)} %copy-done.31) | copy-start | bytes 94564
  618.3 8.4 %copy-start.34 = (f32[985,8]{0,1:T(8,128)S(1)}, f32[985,8]{0,1:T(8,128)}, u32[]{:S(2)}) copy-start(f32[985,8]{0,1:T(8,128)} %copy-done.33) | copy-start | bytes 94564
  618.3 8.4 %copy-start.50 = (bf16[512,8]{0,1:T(8,128)(2,1)S(1)}, bf16[512,8]{0,1:T(8,128)(2,1)}, u32[]{:S(2)}) copy-start(bf16[512,8]{0,1:T(8,128)(2,1)} %copy-done.49) | copy-start | bytes 24580
  618.3 8.4 %copy-start.54 = (f32[4,1,128]{2,1,0:T(1,128)S(1)}, f32[4,1,128]{2,1,0:T(1,128)}, u32[]{:S(2)}) copy-start(f32[4,1,128]{2,1,0:T(1,128)} %copy-done.53) | copy-start | bytes 6148
  618.3 8.4 %copy-start.59 = (f32[985]{0:T(1024)S(1)}, f32[985]{0:T(1024)}, u32[]{:S(2)}) copy-start(f32[985]{0:T(1024)} %copy-done.58) | copy-start | bytes 11824
  636.8 7.1 copy-start.14
  636.8 7.1 copy-start.30
  644.0 16.0 %slice-start = ((s8[8192000]{0:T(1024)(128)(4,1)}), s8[4194304]{0:T(1024)(128)(4,1)S(1)}, s32[]{:S(2)}) async-start(s8[8192000]{0:T(1024)(128)(4,1)} %bitcast.143), calls=%async_computation.21 | async-start | bytes 8388608
  650.7 9.2 %slice-start.1 = ((s8[8192000]{0:T(1024)(128)(4,1)}), s8[3997696]{0:T(1024)(128)(4,1)S(1)}, s32[]{:S(2)}) async-start(s8[8192000]{0:T(1024)(128)(4,1)} %bitcast.143), calls=%async_computation.22 | async-start | bytes 7995392
  662.9 86.2 %reduce-scatter.14.cloned.1.call-start = ((), (), s32[]{:S(2)}) async-start(), calls=%async_computation.13 | async-start | bytes 1966080 | tf_op jit(solution)/shard_map/reduce_scatter | solution.py:289
  666.1 8.2 copy-start.21
  695.2 46.7 %copy-start.75 = (s32[8]{0:T(128)S(1)}, s32[8]{0:T(128)}, u32[]{:S(2)}) copy-start(s32[8]{0:T(128)} %param.34) | copy-start | bytes 100
  695.3 127.8 %all-reduce.13.cloned.1.call-start = ((), (), s32[]{:S(2)}) async-start(), calls=%async_computation.20 | async-start | bytes 1048576 | tf_op jit(solution)/shard_map/psum | solution.py:317
  749.1 33.1 %copy-start.19 = (f32[985,512]{1,0:T(8,128)S(1)}, f32[985,512]{1,0:T(8,128)}, u32[]{:S(2)}) copy-start(f32[985,512]{1,0:T(8,128)} %multiply_add_fusion) | copy-start | bytes 6051844
  749.1 34.7 %copy-start.28 = (bf16[128,1536]{1,0:T(8,128)(2,1)S(1)}, bf16[128,1536]{1,0:T(8,128)(2,1)}, u32[]{:S(2)}) copy-start(bf16[128,1536]{1,0:T(8,128)(2,1)} %param.21) | copy-start | bytes 1179652
  (36 other events, 121.5 us)
Sparse Core Ops, SparseCore 0:
  9.7 22.3 all-gather.10
  33.7 22.6 all-gather.12
  57.9 24.9 all-gather.14
  443.1 20.0 reduce-scatter.25
  476.5 22.0 reduce-scatter.23
  563.8 19.9 reduce-scatter.21
  586.5 31.3 reduce-scatter.19
  620.4 31.4 reduce-scatter.17
  663.0 19.4 reduce-scatter.15
  695.4 26.2 reduce-scatter.13
  749.3 73.7 all-reduce.12
